TPU v7x, 32 devices: a whole 2x2x4 slice. The times are simulated.
32 devices in a mesh: dp: 2 (over x), fsdp: 4 (over z), expert: 4 (over y, core).
Axes of the slice: x: 2, y: 2, z: 4, core: 2. Of those that a mesh axis runs over, the one named last changes fastest.
Arguments:
- window: bfloat16 [256, 4096], P('fsdp'), may hold values from -3 to 3
- attention_gain: float32 [4096], replicated, may hold values from 0.1 to 1.9
- query_weight: bfloat16 [4096, 4096], P('fsdp', 'expert'), may hold values from -0.09375 to 0.09375
- key_weight: bfloat16 [4096, 1024], P('fsdp', 'expert'), may hold values from -0.1875 to 0.1875
- value_weight: bfloat16 [4096, 1024], P('fsdp', 'expert'), may hold values from -0.1875 to 0.1875
- out_weight: bfloat16 [4096, 4096], P('expert', 'fsdp'), may hold values from -0.1875 to 0.1875
- cache_keys: bfloat16 [1024, 1024], P('dp', 'expert'), may hold values from -104 to 104
- cache_values: bfloat16 [1024, 1024], P('dp', 'expert'), may hold values from -12 to 12
- occluded: int32 [1024, 2], P('dp'), may hold values from 0 to 1, as said below
- feedforward_gain: float32 [4096], replicated, may hold values from 0.1 to 1.9
- router_weight: bfloat16 [4096, 4], replicated, may hold values from -0.0234375 to 0.0234375
- chosen_experts: int32 [2, 256, 2], P('dp', 'fsdp'), may hold values from 0 to 3, all different within a row; in each aligned block of 64 rows (0 to 63, 64 to 127, ..., all dimensions but the last counted through in order) at most 64 rows name the same one
- gate_weight: bfloat16 [4, 12288, 4096], P('expert', ('dp', 'fsdp')), may hold values from -0.09375 to 0.09375
- up_weight: bfloat16 [4, 12288, 4096], P('expert', ('dp', 'fsdp')), may hold values from -0.09375 to 0.09375
- down_weight: bfloat16 [4, 12288, 4096], P('expert', ('dp', 'fsdp')), may hold values from -0.0546875 to 0.0546875
Outputs:
- layer_output: bfloat16 [2, 256, 4096], P('dp', 'fsdp')
Inputs may be any that keep to these rules, and one draw needn't show every extreme that they name: `chosen_experts`: each row names 2 different experts. In each aligned block of 64 rows, counting the leading dimensions together (the rows of one device), no expert is named by more than 64 rows, a bound that some block reaches. `occluded`: constant over each aligned run of 64 prefix positions.
All inputs are finite; a program needn't handle non-finite values.
Results may differ from a plain program's by a relative error of at most 0.0095.
The roundings to bfloat16 on the way count: a program that leaves them out, or rounds other values in their place, can miss the bound.
Values may be sent and summed in bfloat16 or wider, within the bound.
A program may use at most 128 MiB of HBM per device.

v0:
```python
import jax
import jax.numpy as jnp
from jax import lax
from jax.sharding import PartitionSpec as P

HD = 128
TOP = 2
epsilon = 1e-05
rope_base = 1000000.0
floor_score = -1e30


def rms_norm(values, scales):
    widened = values.astype(jnp.float32)
    inverse = lax.rsqrt(jnp.mean(widened * widened, axis=-1, keepdims=True) + epsilon)
    return (widened * inverse * scales).astype(jnp.bfloat16)


def rotate(vectors, positions):
    halfway = vectors.shape[-1] // 2
    powers = jnp.arange(halfway, dtype=jnp.float32) * (2.0 / vectors.shape[-1])
    frequency = rope_base ** (-powers)
    angles = positions.astype(jnp.float32)[:, None] * frequency[None, :]
    cosine = jnp.cos(angles)[:, None, :]
    sine_part = jnp.sin(angles)[:, None, :]
    former = vectors[..., :halfway]
    latter = vectors[..., halfway:]
    return jnp.concatenate(
        [former * cosine - latter * sine_part, latter * cosine + former * sine_part], axis=-1
    )


def absorb_block(running, scores, visible, values_block):
    running_top, running_total, running_output = running
    masked = jnp.where(visible, scores, floor_score)
    fresh_top = jnp.maximum(running_top, jnp.max(masked, axis=-1))
    weights = jnp.where(visible, jnp.exp(masked - fresh_top[..., None]), 0.0)
    fresh_total = jnp.sum(weights, axis=-1)
    fresh_output = jnp.einsum(
        "kgtn,nkd->kgtd",
        weights.astype(jnp.bfloat16),
        values_block,
        preferred_element_type=jnp.float32,
    )
    return (fresh_top, fresh_total, fresh_output)


def local(
    window,
    attention_gain,
    query_weight,
    key_weight,
    value_weight,
    out_weight,
    cache_keys,
    cache_values,
    occluded,
    feedforward_gain,
    router_weight,
    chosen_experts,
    gate_weight,
    up_weight,
    down_weight,
):
    token_rows = window.shape[0]
    fsdp_count = lax.axis_size("fsdp")
    fsdp_place = lax.axis_index("fsdp")
    data_place = lax.axis_index("dp")
    expert_place = lax.axis_index("expert")
    query_heads = query_weight.shape[1] // HD
    key_heads = key_weight.shape[1] // HD
    grouping = query_heads // key_heads
    window_rows = token_rows * fsdp_count
    prefix_rows = cache_keys.shape[0] * lax.axis_size("dp")
    score_scale = HD ** (-0.5)
    normed = rms_norm(window, attention_gain)
    first_row = fsdp_place * token_rows
    own_positions = prefix_rows + first_row + jnp.arange(token_rows, dtype=jnp.int32)
    all_positions = prefix_rows + jnp.arange(window_rows, dtype=jnp.int32)
    everyone = lax.all_gather(normed, "fsdp", axis=0, tiled=True)
    slab_width = query_weight.shape[0]
    columns = lax.dynamic_slice_in_dim(everyone, fsdp_place * slab_width, slab_width, 1)
    row_block = columns
    query_sum = lax.psum_scatter(
        jnp.dot(row_block, query_weight, preferred_element_type=jnp.float32),
        "fsdp",
        scatter_dimension=0,
        tiled=True,
    )
    key_sum, value_sum = lax.psum(
        (
            jnp.dot(columns, key_weight, preferred_element_type=jnp.float32),
            jnp.dot(columns, value_weight, preferred_element_type=jnp.float32),
        ),
        "fsdp",
    )
    queries = rotate(query_sum.reshape(token_rows, query_heads, HD), own_positions).astype(
        jnp.bfloat16
    )
    window_keys = (
        rotate(key_sum.reshape(window_rows, key_heads, HD), all_positions)
        .astype(jnp.bfloat16)
        .reshape(window_rows, key_heads * HD)
    )
    window_values = value_sum.astype(jnp.bfloat16)
    query_grid = queries.reshape(token_rows, key_heads, grouping, HD)
    fresh_keys = window_keys.reshape(window_rows, key_heads, HD)
    fresh_values = window_values.reshape(window_rows, key_heads, HD)
    window_scores = (
        jnp.einsum("tkgd,nkd->kgtn", query_grid, fresh_keys, preferred_element_type=jnp.float32)
        * score_scale
    )
    causal = jnp.arange(window_rows)[None, :] <= (first_row + jnp.arange(token_rows))[:, None]
    empty_state = (
        jnp.full((key_heads, grouping, token_rows), floor_score, jnp.float32),
        jnp.zeros((key_heads, grouping, token_rows), jnp.float32),
        jnp.zeros((key_heads, grouping, token_rows, HD), jnp.float32),
    )
    window_state = absorb_block(empty_state, window_scores, causal, fresh_values)
    occluded_flags = occluded.astype(jnp.bfloat16)
    keys_block = lax.all_gather(cache_keys, "dp", axis=0, tiled=True)
    values_block = lax.all_gather(cache_values, "dp", axis=0, tiled=True)
    flags_block = lax.all_gather(occluded_flags, "dp", axis=0, tiled=True)
    block_length = keys_block.shape[0]
    scores = (
        jnp.einsum(
            "tkgd,nkd->kgtn",
            query_grid,
            keys_block.reshape(block_length, key_heads, HD),
            preferred_element_type=jnp.float32,
        )
        * score_scale
    )
    visible = lax.dynamic_slice_in_dim(flags_block, data_place, 1, 1)[:, 0] == 0
    prefix_state = absorb_block(
        empty_state, scores, visible, values_block.reshape(block_length, key_heads, HD)
    )
    overall = jnp.maximum(prefix_state[0], window_state[0])
    prefix_fade = jnp.exp(prefix_state[0] - overall)
    window_fade = jnp.exp(window_state[0] - overall)
    denominator = prefix_state[1] * prefix_fade + window_state[1] * window_fade
    head_values = (
        prefix_state[2] * prefix_fade[..., None] + window_state[2] * window_fade[..., None]
    ) / denominator[..., None]
    attended = (
        head_values.transpose(2, 0, 1, 3).reshape(token_rows, query_heads * HD).astype(jnp.bfloat16)
    )
    head_terms = jnp.dot(
        attended,
        lax.all_gather(out_weight, "fsdp", axis=1, tiled=True),
        preferred_element_type=jnp.float32,
    )
    residual = window.astype(jnp.float32) + lax.psum(head_terms, "expert")
    normed_mix = rms_norm(residual, feedforward_gain)
    logits = jnp.dot(normed_mix, router_weight, preferred_element_type=jnp.float32)
    expert_count = router_weight.shape[1]
    expert_picks = chosen_experts.reshape(token_rows, TOP)
    matches = expert_picks[:, :, None] == jnp.arange(expert_count, dtype=jnp.int32)[None, None, :]
    picked = jnp.sum(jnp.where(matches, logits[:, None, :], 0.0), axis=-1)
    gate_shares = jax.nn.sigmoid(picked - picked[:, ::-1])
    expert_hits = expert_picks == expert_place
    taken_flag = jnp.any(expert_hits, axis=1).astype(jnp.int32)
    weight_mine = jnp.sum(jnp.where(expert_hits, gate_shares, 0.0), axis=1)
    capacity = min(token_rows, 2 * token_rows * TOP // expert_count)
    slot_numbers = jnp.cumsum(taken_flag) - taken_flag
    placing = (slot_numbers[:, None] == jnp.arange(capacity, dtype=jnp.int32)[None, :]) & (
        taken_flag[:, None] == 1
    )
    send_rows = lax.dot_general(
        placing.astype(jnp.bfloat16),
        normed_mix,
        (((0,), (0,)), ((), ())),
        preferred_element_type=jnp.float32,
    ).astype(jnp.bfloat16)
    gate_rows = gate_weight[0]
    up_rows = up_weight[0]
    down_rows = down_weight[0]
    contract_last = (((1,), (1,)), ((), ()))
    piece_rows = lax.all_gather(send_rows, ("dp", "fsdp"), axis=0, tiled=True)
    gate_values = lax.dot_general(
        piece_rows, gate_rows, contract_last, preferred_element_type=jnp.float32
    )
    lifted = lax.dot_general(piece_rows, up_rows, contract_last, preferred_element_type=jnp.float32)
    hidden = (jax.nn.silu(gate_values) * lifted).astype(jnp.bfloat16)
    row_block = hidden
    expert_output = lax.psum_scatter(
        jnp.dot(row_block, down_rows, preferred_element_type=jnp.float32).astype(jnp.bfloat16),
        ("dp", "fsdp"),
        scatter_dimension=0,
        tiled=True,
    ).astype(jnp.float32)
    returned = jnp.dot(
        placing.astype(jnp.float32),
        expert_output,
        precision=lax.Precision.HIGHEST,
        preferred_element_type=jnp.float32,
    )
    mixture = lax.psum(returned * weight_mine[:, None], "expert")
    return (residual + mixture).astype(jnp.bfloat16).reshape(1, token_rows, residual.shape[1])


def solution(mesh):
    placed = (
        P("fsdp", None),
        P(),
        P("fsdp", "expert"),
        P("fsdp", "expert"),
        P("fsdp", "expert"),
        P("expert", "fsdp"),
        P("dp", "expert"),
        P("dp", "expert"),
        P("dp", None),
        P(),
        P(),
        P("dp", "fsdp", None),
        P("expert", ("dp", "fsdp"), None),
        P("expert", ("dp", "fsdp"), None),
        P("expert", ("dp", "fsdp"), None),
    )
    return jax.shard_map(
        local, mesh=mesh, in_specs=placed, out_specs=P("dp", "fsdp", None), check_vma=False
    )
```

profile of v0, /device:TPU:0, one launch (start us, length us, event | category | flops | bytes accessed | tf_op | source)
XLA Modules:
  0.0 560.7 jit_solution(14526967308801473713)
XLA Ops:
  6.5 1.4 fusion.29
  8.0 2.0 fusion.31
  10.1 48.7 %all-gather.4.cloned.1.call-done = bf16[256,4096]{1,0:T(8,128)(2,1)} async-done(((bf16[64,4096]{1,0:T(8,128)(2,1)}), bf16[256,4096]{1,0:T(8,128)(2,1)}) %all-gather.4.cloned.1.call-update) | async-done | bytes 2097168 | tf_op jit(solution)/shard_map/all_gather | solution.py:80
  58.8 1.4 fusion.43
  60.2 0.8 copy.41
  61.1 2.7 fusion.45
  63.9 0.5 all-gather.6.cloned.1.call-update
  64.6 0.3 copy-done.6
  64.8 0.1 copy.37
  65.0 0.1 copy.39
  65.1 4.3 all_gather.18
  69.5 7.9 %all_gather.20 = bf16[1024,256]{0,1:T(8,128)(2,1)S(1)} all-gather(bf16[512,256]{0,1:T(8,128)(2,1)S(1)} %copy.37), channel_id=1, replica_groups=mesh['dp'=2,'fsdp'=4,'expert'=4] {'dp'}, dimensions={0}, use_global_device_ids=true | all-gather | bytes 786432 | tf_op jit(solution)/shard_map/all_gather | solution.py:121
  77.4 7.1 %all_gather.21 = bf16[1024,256]{0,1:T(8,128)(2,1)S(1)} all-gather(bf16[512,256]{0,1:T(8,128)(2,1)S(1)} %copy.39), channel_id=1, replica_groups=mesh['dp'=2,'fsdp'=4,'expert'=4] {'dp'}, dimensions={0}, use_global_device_ids=true | all-gather | bytes 786432 | tf_op jit(solution)/shard_map/all_gather | solution.py:122
  84.5 0.1 iota_compare_fusion
  84.6 0.2 multiply_cosine_fusion.1
  84.8 0.5 multiply_cosine_fusion
  85.3 1.3 fusion.41
  86.7 23.1 %all-reduce.10 = bf16[256,256]{1,0:T(8,128)(2,1)S(1)} all-reduce(f32[256,256]{1,0:T(8,128)S(1)} %fusion.41), channel_id=1, replica_groups=mesh['dp'=2,'fsdp'=4,'expert'=4] {'fsdp'}, use_global_device_ids=true, to_apply=%region_5.6 | all-reduce | flops 65536 | bytes 393216 | tf_op jit(solution)/shard_map/psum | solution.py:90
  109.9 1.2 subtract_convert_fusion
  111.1 14.3 %reduce-scatter.3.cloned.1.call-done = f32[64,1024]{1,0:T(8,128)} async-done(((f32[256,1024]{1,0:T(8,128)}), f32[64,1024]{1,0:T(8,128)}) %reduce-scatter.3.cloned.1.call-update) | async-done | bytes 262160 | tf_op jit(solution)/shard_map/reduce_scatter | solution.py:84
  125.4 1.0 copy.55
  126.4 0.2 subtract_convert_fusion.1
  126.6 0.4 fusion.79
  127.1 0.3 fusion.39
  127.3 0.6 bitcast_reduce_fusion
  127.9 0.6 fusion.20
  128.6 0.6 fusion.27
  129.2 0.3 fusion.28
  129.5 0.1 copy.43
  129.8 145.4 %all-gather.6.cloned.1.call-done = bf16[1024,4096]{1,0:T(8,128)(2,1)} async-done(((bf16[1024,1024]{1,0:T(8,128)(2,1)}), bf16[1024,4096]{1,0:T(8,128)(2,1)}) %all-gather.6.cloned.1.call-update) | async-done | bytes 8388624 | tf_op jit(solution)/shard_map/all_gather | solution.py:150
  275.1 6.0 %fusion.80 = f32[64,4096]{1,0:T(8,128)} fusion(bf16[64,1024]{1,0:T(8,128)(2,1)S(1)} %convert_element_type.96, bf16[1024,4096]{1,0:T(8,128)(2,1)} %all-gather.6.cloned.1.call-done), kind=kOutput, calls=%fused_computation.113 | convolution fusion | flops 536870912 | bytes 9568256 | tf_op jit(solution)/shard_map/dot_general | solution.py:148
  281.3 0.1 copy.44
  281.4 0.1 reduce-window.8
  281.5 0.1 reduce.1
  281.6 34.0 %all-reduce.7.cloned.1.call-done = f32[64,4096]{1,0:T(8,128)} async-done(((f32[64,4096]{1,0:T(8,128)}), f32[64,4096]{1,0:T(8,128)}) %all-reduce.7.cloned.1.call-update) | async-done | bytes 1048592 | tf_op jit(solution)/shard_map/psum | solution.py:153
  315.6 1.6 multiply_reduce_fusion
  317.2 0.2 multiply_convert_fusion
  317.4 1.2 convolution_convert_fusion
  318.7 0.2 reduce-scatter.5.cloned.1.call-start
  318.9 73.7 %all-gather.8.cloned.1.call-done = bf16[512,4096]{1,0:T(8,128)(2,1)} async-done(((bf16[64,4096]{1,0:T(8,128)(2,1)}), bf16[512,4096]{1,0:T(8,128)(2,1)}) %all-gather.8.cloned.1.call-update) | async-done | bytes 4194320 | tf_op jit(solution)/shard_map/all_gather | solution.py:179
  392.6 12.1 %fusion.4 = f32[512,1536]{1,0:T(8,128)} fusion(bf16[512,4096]{1,0:T(8,128)(2,1)} %all-gather.8.cloned.1.call-done, bf16[1,1536,4096]{2,1,0:T(8,128)(2,1)} %param.27), kind=kOutput, calls=%fused_computation.4 | convolution fusion | flops 6442450944 | bytes 19922944 | tf_op jit(solution)/shard_map/dot_general | solution.py:180
  404.7 21.8 %fusion.6 = bf16[512,4096]{1,0:T(8,128)(2,1)} fusion(bf16[1,1536,4096]{2,1,0:T(8,128)(2,1)} %param.29, bf16[512,4096]{1,0:T(8,128)(2,1)} %all-gather.8.cloned.1.call-done, bf16[1,1536,4096]{2,1,0:T(8,128)(2,1)} %param.28, f32[512,1536]{1,0:T(8,128)} %fusion.4), kind=kOutput, calls=%fused_computation.6 | convolution fusion | flops 12891717632 | bytes 36700160 | tf_op jit(solution)/shard_map/dot_general | solution.py:187
  426.6 0.7 copy-done.8
  427.3 0.2 fusion.81
  427.6 85.3 %reduce-scatter.5.cloned.1.call-done = bf16[64,4096]{1,0:T(8,128)(2,1)} async-done(((bf16[512,4096]{1,0:T(8,128)(2,1)}), bf16[64,4096]{1,0:T(8,128)(2,1)}) %reduce-scatter.5.cloned.1.call-update) | async-done | bytes 524304 | tf_op jit(solution)/shard_map/reduce_scatter | solution.py:186
  512.9 2.4 convolution_multiply_fusion
  515.4 36.0 %all-reduce.9.cloned.1.call-done = f32[64,4096]{1,0:T(8,128)} async-done(((f32[64,4096]{1,0:T(8,128)}), f32[64,4096]{1,0:T(8,128)}) %all-reduce.9.cloned.1.call-update) | async-done | bytes 1048592 | tf_op jit(solution)/shard_map/psum | solution.py:198
  551.3 2.5 fusion.38
  (58 shorter events, 0.8 us)
Async XLA Ops:
  6.5 54.6 %copy-start = (bf16[1024,1024]{1,0:T(8,128)(2,1)S(1)}, bf16[1024,1024]{1,0:T(8,128)(2,1)}, u32[]{:S(2)}) copy-start(bf16[1024,1024]{1,0:T(8,128)(2,1)} %param.17) | copy-start | bytes 6291460
  6.5 52.3 %copy-start.4 = (bf16[1024,256]{1,0:T(8,128)(2,1)S(1)}, bf16[1024,256]{1,0:T(8,128)(2,1)}, u32[]{:S(2)}) copy-start(bf16[1024,256]{1,0:T(8,128)(2,1)} %param.18) | copy-start | bytes 1572868
  6.5 52.3 %all-gather.4.cloned.1.call-start = ((), (), s32[]{:S(2)}) async-start(), calls=%async_computation.2 | async-start | bytes 2621440 | tf_op jit(solution)/shard_map/all_gather | solution.py:80
  10.0 99.9 %all-reduce.5.cloned.1.call-start = ((), (), s32[]{:S(2)}) async-start(), calls=%async_computation.4 | async-start | bytes 524288 | tf_op jit(solution)/shard_map/psum | solution.py:90
  61.1 64.4 %reduce-scatter.3.cloned.1.call-start = ((), (), s32[]{:S(2)}) async-start(), calls=%async_computation.3 | async-start | bytes 1310720 | tf_op jit(solution)/shard_map/reduce_scatter | solution.py:84
  63.9 0.7 copy-start.11
  63.9 1.0 copy-start.6
  63.9 1.1 copy-start.7
  63.9 21.4 %copy-start.5 = (bf16[1024,256]{1,0:T(8,128)(2,1)S(1)}, bf16[1024,256]{1,0:T(8,128)(2,1)}, u32[]{:S(2)}) copy-start(bf16[1024,256]{1,0:T(8,128)(2,1)} %param.19) | copy-start | bytes 1572868
  63.9 211.2 %all-gather.6.cloned.1.call-start = ((), (), s32[]{:S(2)}) async-start(), calls=%async_computation.5 | async-start | bytes 10485760 | tf_op jit(solution)/shard_map/all_gather | solution.py:150
  64.5 251.1 %all-reduce.7.cloned.1.call-start = ((), (), s32[]{:S(2)}) async-start(), calls=%async_computation.6 | async-start | bytes 2097152 | tf_op jit(solution)/shard_map/psum | solution.py:153
  129.7 151.5 %copy-start.10 = (s32[1,64,2]{1,2,0:T(2,128)S(1)}, s32[1,64,2]{1,2,0:T(2,128)}, u32[]{:S(2)}) copy-start(s32[1,64,2]{1,2,0:T(2,128)} %param.26) | copy-start | bytes 1540
  129.7 185.9 %copy-start.2 = (bf16[64,4096]{1,0:T(8,128)(2,1)S(1)}, bf16[64,4096]{1,0:T(8,128)(2,1)}, u32[]{:S(2)}) copy-start(bf16[64,4096]{1,0:T(8,128)(2,1)} %param.15) | copy-start | bytes 1572868
  281.2 36.0 %copy-start.9 = (f32[4096]{0:T(1024)S(1)}, f32[4096]{0:T(1024)}, u32[]{:S(2)}) copy-start(f32[4096]{0:T(1024)} %param.24) | copy-start | bytes 49156
  281.2 111.4 %all-gather.8.cloned.1.call-start = ((), (), s32[]{:S(2)}) async-start(), calls=%async_computation.7 | async-start | bytes 4718592 | tf_op jit(solution)/shard_map/all_gather | solution.py:179
  315.6 1.6 copy-start.3
  318.7 194.2 %reduce-scatter.5.cloned.1.call-start = ((), (), s32[]{:S(2)}) async-start(), calls=%async_computation.8 | async-start | bytes 4718592 | tf_op jit(solution)/shard_map/reduce_scatter | solution.py:186
  426.5 0.8 copy-start.8
  426.5 124.8 %all-reduce.9.cloned.1.call-start = ((), (), s32[]{:S(2)}) async-start(), calls=%async_computation.9 | async-start | bytes 2097152 | tf_op jit(solution)/shard_map/psum | solution.py:198
  515.3 38.5 %copy-start.1 = (bf16[1024,1024]{1,0:T(8,128)(2,1)S(1)}, bf16[1024,1024]{1,0:T(8,128)(2,1)}, u32[]{:S(2)}) copy-start(bf16[1024,1024]{1,0:T(8,128)(2,1)} %param.17) | copy-start | bytes 6291460
Sparse Core Ops, SparseCore 0:
  10.1 48.6 all-gather.3
  61.2 34.6 all-reduce.4
  98.2 27.1 reduce-scatter.2
  126.8 148.2 all-gather.5
  281.3 34.2 all-reduce.6
  318.8 73.7 all-gather.7
  426.7 86.1 reduce-scatter.4
  515.5 35.8 all-reduce.8
where the time goes:
time: 561 us
  waiting for transfers between devices  438 us (78%)
  matrix products  51.2 us (9%)
  blocking collectives  42.4 us (8%)
  between operations  13.8 us (2%)
  other arithmetic  11.1 us (2%)
    all_gather x1, waiting for transfers between devices, local(): lax.all_gather(out_weight, 'fsdp', axis=1, tiled=True)  145 us
    reduce_scatter x1, waiting for transfers between devices, local(): lax.psum_scatter(jnp.dot(row_block, down_rows, preferred_element_type=jnp...  85.3 us
    all_gather x1, waiting for transfers between devices, local(): piece_rows = lax.all_gather(send_rows, ('dp', 'fsdp'), axis=0, tiled=True)  73.7 us
    all_gather x1, waiting for transfers between devices, local(): everyone = lax.all_gather(normed, 'fsdp', axis=0, tiled=True)  48.7 us
    psum x1, waiting for transfers between devices, local(): mixture = lax.psum(returned * weight_mine[:, None], 'expert')  36 us
    psum x1, waiting for transfers between devices, local(): residual = window.astype(jnp.float32) + lax.psum(head_terms, 'expert')  34 us
    psum x1, blocking collectives, local(): lax.psum((jnp.dot(columns, key_weight, preferred_element_type=jnp.float32...  23.1 us
    dot_general x1, matrix products, local(): jnp.dot(row_block, down_rows, preferred_element_type=jnp.float32)  21.8 us
  transfers between devices with their start and end apart: 8, of which 7 were waited for; matrix products, arithmetic and copies ran while one was open for 2% of the time, Pallas kernels for 0%

commit v1 on v0

--- a/solution.py
+++ b/solution.py
@@ -118,8 +118,11 @@
     )
     window_state = absorb_block(empty_state, window_scores, causal, fresh_values)
     occluded_flags = occluded.astype(jnp.bfloat16)
-    keys_block = lax.all_gather(cache_keys, "dp", axis=0, tiled=True)
-    values_block = lax.all_gather(cache_values, "dp", axis=0, tiled=True)
+    keys_block, values_block = jnp.split(
+        lax.all_gather(jnp.concatenate([cache_keys, cache_values], 1), "dp", axis=0, tiled=True),
+        [cache_keys.shape[1]],
+        1,
+    )
     flags_block = lax.all_gather(occluded_flags, "dp", axis=0, tiled=True)
     block_length = keys_block.shape[0]
     scores = (

time: 561 us -> 584 us (1.041)
  waiting for transfers between devices: 438 us -> 471 us
  blocking collectives: 42.4 us -> 30.8 us
    all_gather x2 -> x0, blocking collectives: 15 us -> none  [the longest x1 7.89 us: local(): keys_block = lax.all_gather(cache_keys, 'dp', axis=0, tiled=True)]
    reduce_scatter x1, waiting for transfers between devices: 14.3 us -> 28 us  [local(): lax.psum_scatter(jnp.dot(row_block, query_weight, preferred_element_type=...]
    all_gather x0 -> x1, waiting for transfers between devices: none -> 10.6 us  [local(): lax.all_gather(jnp.concatenate([cache_keys, cache_values], 1), 'dp', axis...]
    psum x1, waiting for transfers between devices: 0.02 us -> 9.82 us  [local(): lax.psum((jnp.dot(columns, key_weight, preferred_element_type=jnp.float32...]
  transfers between devices with their start and end apart: 8 -> 9, of which waited for: 7 -> 9; matrix products, arithmetic and copies ran while one was open for 2% -> 3% of each run, Pallas kernels for 0% -> 0%
where the time goes in v1:
time: 584 us
  waiting for transfers between devices  471 us (81%)
  matrix products  51.2 us (9%)
  blocking collectives  30.8 us (5%)
  between operations  13.5 us (2%)
  other arithmetic  12 us (2%)
    all_gather x1, waiting for transfers between devices, local(): lax.all_gather(out_weight, 'fsdp', axis=1, tiled=True)  145 us
    reduce_scatter x1, waiting for transfers between devices, local(): lax.psum_scatter(jnp.dot(row_block, down_rows, preferred_element_type=jnp...  85.5 us
    all_gather x1, waiting for transfers between devices, local(): piece_rows = lax.all_gather(send_rows, ('dp', 'fsdp'), axis=0, tiled=True)  73.7 us
    all_gather x1, waiting for transfers between devices, local(): everyone = lax.all_gather(normed, 'fsdp', axis=0, tiled=True)  47.5 us
    psum x1, waiting for transfers between devices, local(): mixture = lax.psum(returned * weight_mine[:, None], 'expert')  36 us
    psum x1, waiting for transfers between devices, local(): residual = window.astype(jnp.float32) + lax.psum(head_terms, 'expert')  34.1 us
    reduce_scatter x1, waiting for transfers between devices, local(): lax.psum_scatter(jnp.dot(row_block, query_weight, preferred_element_type=...  28 us
    psum x1, blocking collectives, local(): lax.psum((jnp.dot(columns, key_weight, preferred_element_type=jnp.float32...  26.4 us
  transfers between devices with their start and end apart: 9, of which 9 were waited for; matrix products, arithmetic and copies ran while one was open for 3% of the time, Pallas kernels for 0%

profile of v1, /device:TPU:0, one launch (start us, length us, event | category | flops | bytes accessed | tf_op | source)
XLA Modules:
  0.0 583.7 jit_solution(5739063835538089802)
XLA Ops:
  6.5 1.4 fusion.29
  8.0 2.1 fusion.31
  10.1 0.1 copy.35
  10.3 0.1 copy.36
  10.4 0.8 pad_maximum_fusion
  11.4 47.5 %all-gather.7.cloned.1.call-done = bf16[256,4096]{1,0:T(8,128)(2,1)} async-done(((bf16[64,4096]{1,0:T(8,128)(2,1)}), bf16[256,4096]{1,0:T(8,128)(2,1)}) %all-gather.7.cloned.1.call-update) | async-done | bytes 2097168 | tf_op jit(solution)/shard_map/all_gather | solution.py:80
  58.9 1.4 fusion.43
  60.3 0.9 copy.41
  61.2 2.7 fusion.45
  64.0 0.5 all-gather.9.cloned.1.call-update
  64.6 4.3 all_gather.15
  69.1 0.2 multiply_cosine_fusion.1
  69.3 0.5 multiply_cosine_fusion
  69.9 10.6 %all-gather.5.cloned.1.call-done = bf16[1024,512]{0,1:T(8,128)(2,1)} async-done(((bf16[512,512]{0,1:T(8,128)(2,1)}), bf16[1024,512]{0,1:T(8,128)(2,1)}) %all-gather.5.cloned.1.call-update) | async-done | bytes 1048592 | tf_op jit(solution)/shard_map/all_gather | solution.py:122
  80.5 1.3 fusion.79
  81.7 1.3 fusion.41
  83.1 26.4 %all-reduce.10 = bf16[256,256]{1,0:T(8,128)(2,1)S(1)} all-reduce(f32[256,256]{1,0:T(8,128)S(1)} %fusion.41), channel_id=1, replica_groups=mesh['dp'=2,'fsdp'=4,'expert'=4] {'fsdp'}, use_global_device_ids=true, to_apply=%region_5.6 | all-reduce | flops 65536 | bytes 393216 | tf_op jit(solution)/shard_map/psum | solution.py:90
  109.6 9.8 %all-reduce.5.cloned.1.call-done = f32[256,2,128]{2,0,1:T(8,128)} async-done(((f32[256,2,128]{2,0,1:T(8,128)}), f32[256,2,128]{2,0,1:T(8,128)}) %all-reduce.5.cloned.1.call-update) | async-done | bytes 262160 | tf_op jit(solution)/shard_map/psum | solution.py:90
  119.4 1.2 subtract_convert_fusion
  120.6 28.0 %reduce-scatter.3.cloned.1.call-done = f32[64,1024]{1,0:T(8,128)} async-done(((f32[256,1024]{1,0:T(8,128)}), f32[64,1024]{1,0:T(8,128)}) %reduce-scatter.3.cloned.1.call-update) | async-done | bytes 262160 | tf_op jit(solution)/shard_map/reduce_scatter | solution.py:84
  148.6 1.0 copy.55
  149.6 0.2 subtract_convert_fusion.1
  149.8 0.4 fusion.80
  150.2 0.3 fusion.39
  150.5 0.6 bitcast_reduce_fusion
  151.1 0.6 fusion.20
  151.8 0.6 fusion.27
  152.4 0.3 fusion.28
  152.7 0.1 copy.43
  152.9 145.4 %all-gather.9.cloned.1.call-done = bf16[1024,4096]{1,0:T(8,128)(2,1)} async-done(((bf16[1024,1024]{1,0:T(8,128)(2,1)}), bf16[1024,4096]{1,0:T(8,128)(2,1)}) %all-gather.9.cloned.1.call-update) | async-done | bytes 8388624 | tf_op jit(solution)/shard_map/all_gather | solution.py:153
  298.3 6.0 %fusion.81 = f32[64,4096]{1,0:T(8,128)} fusion(bf16[64,1024]{1,0:T(8,128)(2,1)S(1)} %convert_element_type.96, bf16[1024,4096]{1,0:T(8,128)(2,1)} %all-gather.9.cloned.1.call-done), kind=kOutput, calls=%fused_computation.115 | convolution fusion | flops 536870912 | bytes 9568256 | tf_op jit(solution)/shard_map/dot_general | solution.py:151
  304.5 0.1 copy.44
  304.6 0.1 reduce-window.8
  304.6 0.1 reduce.1
  304.8 34.1 %all-reduce.7.cloned.1.call-done = f32[64,4096]{1,0:T(8,128)} async-done(((f32[64,4096]{1,0:T(8,128)}), f32[64,4096]{1,0:T(8,128)}) %all-reduce.7.cloned.1.call-update) | async-done | bytes 1048592 | tf_op jit(solution)/shard_map/psum | solution.py:156
  338.8 1.6 multiply_reduce_fusion
  340.4 0.2 multiply_convert_fusion
  340.6 1.2 convolution_convert_fusion
  341.9 0.2 reduce-scatter.5.cloned.1.call-start
  342.1 73.7 %all-gather.11.cloned.1.call-done = bf16[512,4096]{1,0:T(8,128)(2,1)} async-done(((bf16[64,4096]{1,0:T(8,128)(2,1)}), bf16[512,4096]{1,0:T(8,128)(2,1)}) %all-gather.11.cloned.1.call-update) | async-done | bytes 4194320 | tf_op jit(solution)/shard_map/all_gather | solution.py:182
  415.8 12.2 %fusion.4 = f32[512,1536]{1,0:T(8,128)} fusion(bf16[512,4096]{1,0:T(8,128)(2,1)} %all-gather.11.cloned.1.call-done, bf16[1,1536,4096]{2,1,0:T(8,128)(2,1)} %param.27), kind=kOutput, calls=%fused_computation.4 | convolution fusion | flops 6442450944 | bytes 19922944 | tf_op jit(solution)/shard_map/dot_general | solution.py:183
  427.9 21.8 %fusion.6 = bf16[512,4096]{1,0:T(8,128)(2,1)} fusion(bf16[1,1536,4096]{2,1,0:T(8,128)(2,1)} %param.29, bf16[512,4096]{1,0:T(8,128)(2,1)} %all-gather.11.cloned.1.call-done, bf16[1,1536,4096]{2,1,0:T(8,128)(2,1)} %param.28, f32[512,1536]{1,0:T(8,128)} %fusion.4), kind=kOutput, calls=%fused_computation.6 | convolution fusion | flops 12891717632 | bytes 36700160 | tf_op jit(solution)/shard_map/dot_general | solution.py:190
  449.8 0.7 copy-done.8
  450.5 0.2 fusion.82
  450.8 85.5 %reduce-scatter.5.cloned.1.call-done = bf16[64,4096]{1,0:T(8,128)(2,1)} async-done(((bf16[512,4096]{1,0:T(8,128)(2,1)}), bf16[64,4096]{1,0:T(8,128)(2,1)}) %reduce-scatter.5.cloned.1.call-update) | async-done | bytes 524304 | tf_op jit(solution)/shard_map/reduce_scatter | solution.py:189
  536.3 2.4 convolution_multiply_fusion
  538.7 36.0 %all-reduce.9.cloned.1.call-done = f32[64,4096]{1,0:T(8,128)} async-done(((f32[64,4096]{1,0:T(8,128)}), f32[64,4096]{1,0:T(8,128)}) %all-reduce.9.cloned.1.call-update) | async-done | bytes 1048592 | tf_op jit(solution)/shard_map/psum | solution.py:201
  574.7 2.5 fusion.38
  (61 shorter events, 0.9 us)
Async XLA Ops:
  6.5 54.7 %copy-start = (bf16[1024,1024]{1,0:T(8,128)(2,1)S(1)}, bf16[1024,1024]{1,0:T(8,128)(2,1)}, u32[]{:S(2)}) copy-start(bf16[1024,1024]{1,0:T(8,128)(2,1)} %param.17) | copy-start | bytes 6291460
  6.5 3.6 copy-start.6
  6.5 3.7 copy-start.7
  6.5 52.3 %all-gather.7.cloned.1.call-start = ((), (), s32[]{:S(2)}) async-start(), calls=%async_computation.3 | async-start | bytes 2621440 | tf_op jit(solution)/shard_map/all_gather | solution.py:80
  8.0 50.9 %copy-start.4 = (bf16[1024,256]{1,0:T(8,128)(2,1)S(1)}, bf16[1024,256]{1,0:T(8,128)(2,1)}, u32[]{:S(2)}) copy-start(bf16[1024,256]{1,0:T(8,128)(2,1)} %param.18) | copy-start | bytes 1572868
  10.1 70.4 %all-gather.5.cloned.1.call-start = ((), (), s32[]{:S(2)}) async-start(), calls=%async_computation.2 | async-start | bytes 1572864 | tf_op jit(solution)/shard_map/all_gather | solution.py:122
  11.3 108.1 %all-reduce.5.cloned.1.call-start = ((), (), s32[]{:S(2)}) async-start(), calls=%async_computation.5 | async-start | bytes 524288 | tf_op jit(solution)/shard_map/psum | solution.py:90
  61.1 87.4 %reduce-scatter.3.cloned.1.call-start = ((), (), s32[]{:S(2)}) async-start(), calls=%async_computation.4 | async-start | bytes 1310720 | tf_op jit(solution)/shard_map/reduce_scatter | solution.py:84
  63.9 0.7 copy-start.11
  64.0 17.8 %copy-start.5 = (bf16[1024,256]{1,0:T(8,128)(2,1)S(1)}, bf16[1024,256]{1,0:T(8,128)(2,1)}, u32[]{:S(2)}) copy-start(bf16[1024,256]{1,0:T(8,128)(2,1)} %param.19) | copy-start | bytes 1572868
  64.0 234.3 %all-gather.9.cloned.1.call-start = ((), (), s32[]{:S(2)}) async-start(), calls=%async_computation.6 | async-start | bytes 10485760 | tf_op jit(solution)/shard_map/all_gather | solution.py:153
  64.6 274.3 %all-reduce.7.cloned.1.call-start = ((), (), s32[]{:S(2)}) async-start(), calls=%async_computation.7 | async-start | bytes 2097152 | tf_op jit(solution)/shard_map/psum | solution.py:156
  152.9 151.5 %copy-start.10 = (s32[1,64,2]{1,2,0:T(2,128)S(1)}, s32[1,64,2]{1,2,0:T(2,128)}, u32[]{:S(2)}) copy-start(s32[1,64,2]{1,2,0:T(2,128)} %param.26) | copy-start | bytes 1540
  152.9 185.9 %copy-start.2 = (bf16[64,4096]{1,0:T(8,128)(2,1)S(1)}, bf16[64,4096]{1,0:T(8,128)(2,1)}, u32[]{:S(2)}) copy-start(bf16[64,4096]{1,0:T(8,128)(2,1)} %param.15) | copy-start | bytes 1572868
  304.3 36.1 %copy-start.9 = (f32[4096]{0:T(1024)S(1)}, f32[4096]{0:T(1024)}, u32[]{:S(2)}) copy-start(f32[4096]{0:T(1024)} %param.24) | copy-start | bytes 49156
  304.4 111.4 %all-gather.11.cloned.1.call-start = ((), (), s32[]{:S(2)}) async-start(), calls=%async_computation.8 | async-start | bytes 4718592 | tf_op jit(solution)/shard_map/all_gather | solution.py:182
  338.8 1.6 copy-start.3
  341.9 194.4 %reduce-scatter.5.cloned.1.call-start = ((), (), s32[]{:S(2)}) async-start(), calls=%async_computation.9 | async-start | bytes 4718592 | tf_op jit(solution)/shard_map/reduce_scatter | solution.py:189
  449.7 0.8 copy-start.8
  449.8 125.0 %all-reduce.9.cloned.1.call-start = ((), (), s32[]{:S(2)}) async-start(), calls=%async_computation.10 | async-start | bytes 2097152 | tf_op jit(solution)/shard_map/psum | solution.py:201
  538.7 38.5 %copy-start.1 = (bf16[1024,1024]{1,0:T(8,128)(2,1)S(1)}, bf16[1024,1024]{1,0:T(8,128)(2,1)}, u32[]{:S(2)}) copy-start(bf16[1024,1024]{1,0:T(8,128)(2,1)} %param.17) | copy-start | bytes 6291460
Sparse Core Ops, SparseCore 0:
  10.2 48.6 all-gather.6
  60.4 20.0 all-gather.4
  82.8 36.5 all-reduce.4
  121.7 26.8 reduce-scatter.2
  150.0 148.2 all-gather.8
  304.5 34.2 all-reduce.6
  342.0 73.7 all-gather.10
  449.9 86.3 reduce-scatter.4
  538.9 35.8 all-reduce.8
